TPU v7x, 256 devices: a whole 4x4x8 slice. The times are simulated.
256 devices in a mesh: rows: 32 (over x, z_hi, core), mask: 8 (over z_lo, y).
Axes of the slice: x: 4, y: 4, z: 8 (z_hi: 4, z_lo: 2; z = z_hi * 2 + z_lo), core: 2. Of those that a mesh axis runs over, the one named last changes fastest.
Arguments:
- image_field: bfloat16 [2, 8192, 8192], P(None, ('rows', 'mask')), may hold values from -6 to 6
- amplitudes: bfloat16 [8, 8192, 8192], P('mask', None, 'rows'), may hold values from 0 to 12, as said below
- mask_ids: int32 [8], P('mask'), may hold values from 0 to 63
Outputs:
- gradient: float32 [2, 8192, 8192], P(None, ('rows', 'mask'))
- loss_value: float32 [], replicated
Inputs may be any that keep to these rules, and one draw needn't show every extreme that they name: `amplitudes`: magnitudes are non-negative.
All inputs are finite; a program needn't handle non-finite values.
Results may differ from a plain program's by a relative error of at most 0.024.
Values may be sent and summed in bfloat16 or wider, within the bound.
A program may use at most 128 MiB of HBM per device.

v0:
```python
import math
import jax
import jax.numpy as jnp
from jax import lax
from jax.sharding import PartitionSpec as P

INNER = 128
EPSILON = 0.25


def shift_bits(values, count):
    return lax.shift_right_logical(values, jnp.full(values.shape, count, jnp.int32))


def mask_code(window_id, row_index, column_index):
    mixed = (
        row_index * jnp.int32(73856093)
        ^ column_index * jnp.int32(19349663)
        ^ (window_id + jnp.int32(1)) * jnp.int32(83492791)
    )
    mixed = mixed ^ shift_bits(mixed, 13)
    mixed = mixed * jnp.int32(1274126177)
    mixed = mixed ^ shift_bits(mixed, 16)
    return shift_bits(mixed, 28) & jnp.int32(3)


def rotate(real_part, imag_part, phase_code, direction):
    cosine = (phase_code == 0).astype(jnp.float32) - (phase_code == 2).astype(jnp.float32)
    sine = direction * (
        (phase_code == 1).astype(jnp.float32) - (phase_code == 3).astype(jnp.float32)
    )
    return (real_part * cosine - imag_part * sine, real_part * sine + imag_part * cosine)


def factor_table(length, direction):
    index = jnp.arange(length, dtype=jnp.int32)
    angles = (index[:, None] * index[None, :] % length).astype(jnp.float32) * (
        2.0 * math.pi / length
    )
    cosine = jnp.cos(angles)
    sine = direction * jnp.sin(angles)
    upper = jnp.stack([cosine, -sine], axis=1)
    lower = jnp.stack([sine, cosine], axis=1)
    return jnp.stack([upper, lower]).astype(jnp.bfloat16)


def turn_table(outer, inner, length, direction):
    first = jnp.arange(outer, dtype=jnp.int32)[:, None]
    second = jnp.arange(inner, dtype=jnp.int32)[None, :]
    angles = (first * second % length).astype(jnp.float32) * (2.0 * math.pi / length)
    return (jnp.cos(angles), direction * jnp.sin(angles))


def factor(form, table, values):
    return jnp.einsum(form, table, values, preferred_element_type=jnp.float32)


def twist(real_part, imag_part, cosine, sine, axis):
    return jnp.stack(
        [real_part * cosine - imag_part * sine, real_part * sine + imag_part * cosine], axis=axis
    ).astype(jnp.bfloat16)


def rows_forward(values, tables):
    lead_table, sub_table, cosine, sine = tables
    batch, parts, count, length = values.shape
    view = values.reshape(batch, parts, count, lead_table.shape[1], sub_table.shape[1])
    first = factor("pkqj,xqrjb->xprkb", lead_table, view)
    middle = twist(first[:, 0], first[:, 1], cosine, sine, 1)
    second = factor("pkqj,xqraj->xprak", sub_table, middle)
    return second.reshape(batch, parts, count, length) * (1.0 / math.sqrt(length))


def rows_inverse(values, tables):
    lead_table, sub_table, cosine, sine = tables
    batch, parts, count, length = values.shape
    view = values.reshape(batch, parts, count, lead_table.shape[1], sub_table.shape[1])
    first = factor("pkqj,xqraj->xprak", sub_table, view)
    middle = twist(first[:, 0], first[:, 1], cosine, sine, 1)
    second = factor("pkqj,xqrjb->xprkb", lead_table, middle)
    return second.reshape(batch, parts, count, length) * (1.0 / math.sqrt(length))


def cols_forward(values, tables):
    lead_table, sub_table, cosine, sine = tables
    parts, length, width = values.shape
    view = values.reshape(parts, lead_table.shape[1], sub_table.shape[1], width)
    first = factor("pkqj,qjbw->pkbw", lead_table, view)
    middle = twist(first[0], first[1], cosine[:, :, None], sine[:, :, None], 0)
    second = factor("pkqj,qajw->pakw", sub_table, middle)
    return second.reshape(parts, length, width) * (1.0 / math.sqrt(length))


def cols_inverse(values, tables):
    lead_table, sub_table, cosine, sine = tables
    parts, length, width = values.shape
    view = values.reshape(parts, lead_table.shape[1], sub_table.shape[1], width)
    first = factor("pkqj,qajw->pakw", sub_table, view)
    middle = twist(first[0], first[1], cosine[:, :, None], sine[:, :, None], 0)
    second = factor("pkqj,qjbw->pkbw", lead_table, middle)
    return second.reshape(parts, length, width) * (1.0 / math.sqrt(length))


def shards(image_field, amplitudes, mask_ids):
    slab = lax.all_gather(image_field, "mask", axis=1, tiled=True)
    slab_rows = slab.shape[1]
    width = slab.shape[2]
    outer = width // INNER
    forward_cos, forward_sin = turn_table(outer, INNER, width, -1.0)
    inverse_cos, inverse_sin = turn_table(outer, INNER, width, 1.0)
    forward_tables = (
        factor_table(outer, -1.0),
        factor_table(INNER, -1.0),
        forward_cos,
        forward_sin,
    )
    inverse_tables = (factor_table(outer, 1.0), factor_table(INNER, 1.0), inverse_cos, inverse_sin)
    first_row = lax.axis_index("rows") * slab_rows
    row_index = first_row + jnp.arange(slab_rows, dtype=jnp.int32)[:, None]
    column_index = jnp.arange(width, dtype=jnp.int32)[None, :]
    phase_code = mask_code(mask_ids[0], row_index, column_index)
    masked_real, masked_imag = rotate(
        slab[0].astype(jnp.float32), slab[1].astype(jnp.float32), phase_code, 1.0
    )
    masked = jnp.stack([masked_real, masked_imag]).astype(jnp.bfloat16)
    outgoing = rows_forward(masked[None], forward_tables)[0].astype(jnp.bfloat16)
    column_slab = lax.all_to_all(outgoing, "rows", split_axis=2, concat_axis=1, tiled=True)
    spectrum = cols_forward(column_slab, forward_tables)
    spec_real = spectrum[0]
    spec_imag = spectrum[1]
    measured = amplitudes[0].astype(jnp.float32)
    magnitude = jnp.sqrt(spec_real * spec_real + spec_imag * spec_imag + EPSILON)
    factor_kept = 1.0 - measured / magnitude
    misfit = magnitude - measured
    loss_part = jnp.sum(misfit * misfit)
    weighted = jnp.stack([spec_real * factor_kept, spec_imag * factor_kept]).astype(jnp.bfloat16)
    returning = cols_inverse(weighted, inverse_tables).astype(jnp.bfloat16)
    row_slab = lax.all_to_all(returning, "rows", split_axis=1, concat_axis=2, tiled=True)
    back = rows_inverse(row_slab[None], inverse_tables)[0]
    term_real, term_imag = rotate(back[0], back[1], phase_code, -1.0)
    gradient = lax.psum_scatter(
        jnp.stack([term_real, term_imag]).astype(jnp.bfloat16),
        "mask",
        scatter_dimension=1,
        tiled=True,
    ).astype(jnp.float32)
    loss_total = lax.psum(loss_part, ("rows", "mask"))
    loss_value = loss_total / (lax.axis_size("mask") * width * width)
    return (gradient, loss_value)


def solution(mesh):
    return jax.shard_map(
        shards,
        mesh=mesh,
        in_specs=(P(None, ("rows", "mask"), None), P("mask", None, "rows"), P("mask")),
        out_specs=(P(None, ("rows", "mask"), None), P()),
        check_vma=False,
    )
```

profile of v0, /device:TPU:1, one launch (start us, length us, event | category | flops | bytes accessed | tf_op | source)
XLA Modules:
  0.0 996.1 jit_solution(3554799397838370587)
XLA Ops:
  10.1 98.1 %all-gather.2.cloned.1.call-done = bf16[2,256,8192]{2,1,0:T(8,128)(2,1)} async-done(((bf16[2,32,8192]{2,1,0:T(8,128)(2,1)}), bf16[2,256,8192]{2,1,0:T(8,128)(2,1)}) %all-gather.2.cloned.1.call-update) | async-done | bytes 8388624 | tf_op jit(solution)/shard_map/all_gather | solution.py:105
  108.2 9.7 fusion.49
  139.2 16.8 %fusion.41 = bf16[1,2,256,64,128]{2,4,1,3,0:T(8,128)(2,1)} fusion(bf16[2,256,64,128,1]{3,2,1,0,4:T(8,128)(2,1)} %maximum_bitcast_fusion.2, bf16[1,128,2,128]{3,1,2,0:T(8,128)(2,1)S(1)} %get-tuple-element.21, bf16[1,128,2,128]{3,1,2,0:T(8,128)(2,1)S(1)} %get-tuple-element.22), kind=kOutput, calls=%fused_computation.77 | convolution fusion | flops 2156134400 | bytes 16908288 | tf_op jit(solution)/shard_map/pkqj,xqraj->xprak/dot_general | solution.py:55
  156.0 7.7 copy.71
  163.7 16.4 %copy.72 = bf16[2,256,8192]{1,0,2:T(2,128)(2,1)} copy(bf16[2,256,8192]{1,2,0:T(8,128)(2,1)} %bitcast.205) | data formatting | bytes 16777216 | tf_op jit(solution)/shard_map/convert_element_type | solution.py:126
  180.1 9.4 all-to-all-start
  190.5 148.9 %all-to-all-done = bf16[2,256,8192]{1,0,2:T(2,128)(2,1)} async-done(((bf16[2,256,8192]{1,0,2:T(2,128)(2,1)}), bf16[2,256,8192]{1,0,2:T(2,128)(2,1)}, u32[]{:S(2)}, u32[]{:S(2)}) %all-to-all-start) | async-done | bytes 8388640 | tf_op jit(solution)/shard_map/all_to_all | solution.py:127
  339.4 7.7 copy.73
  347.1 12.0 %copy.74 = bf16[2,32,256,256]{3,2,1,0:T(8,128)(2,1)} copy(bf16[2,32,256,256]{2,3,1,0:T(8,128)(2,1)} %bitcast.206) | data formatting | bytes 16777216 | tf_op jit(solution)/shard_map/all_to_all | solution.py:127
  359.1 9.7 fusion.36
  380.4 10.0 %fusion.2 = f32[2,64,128,256]{3,2,0,1:T(8,128)S(1)} fusion(bf16[2,64,128,256,1]{3,1,2,0,4:T(8,128)(2,1)} %maximum_bitcast_fusion.3, bf16[1,128,2,128]{3,1,2,0:T(8,128)(2,1)S(1)} %get-tuple-element.21, bf16[1,128,2,128]{3,1,2,0:T(8,128)(2,1)S(1)} %get-tuple-element.22), kind=kOutput, calls=%fused_computation.5 | convolution fusion | flops 2151940096 | bytes 25296896 | tf_op jit(solution)/shard_map/pkqj,qajw->pakw/dot_general | solution.py:55
  397.0 12.9 %fusion.10 = (f32[]{:T(128)}, bf16[1,8192,256]{2,1,0:T(8,128)(2,1)}, bf16[1,8192,256]{2,1,0:T(8,128)(2,1)}) fusion(bf16[1,8192,256]{2,1,0:T(8,128)(2,1)S(1)} %copy-done, f32[1,8192,256]{2,1,0:T(8,128)} %bitcast.211, f32[1,8192,256]{2,1,0:T(8,128)} %bitcast.210), kind=kLoop, calls=%fused_computation.24 | loop fusion | flops 29360128 | bytes 29360132 | tf_op jit(solution)/shard_map/reduce_sum | solution.py:135
  422.7 11.6 %convolution_bitcast_fusion.1 = f32[64,256,2,128]{3,1,2,0:T(8,128)} fusion(bf16[1,64,128,256]{2,3,0,1:T(8,128)(2,1)} %copy.80, bf16[1,64,128,256]{2,3,0,1:T(8,128)(2,1)} %copy.79, bf16[1,128,2,128]{3,1,2,0:T(8,128)(2,1)S(1)} %get-tuple-element.20, bf16[1,128,2,128]{3,1,2,0:T(8,128)(2,1)S(1)} %get-tuple-element.19), kind=kOutput, calls=%fused_computation.17 | convolution fusion | flops 2164523008 | bytes 25296896 | tf_op jit(solution)/shard_map/pkqj,qajw->pakw/dot_general | solution.py:55
  434.2 17.4 %copy.81 = f32[64,256,2,128]{1,0,3,2:T(8,128)} copy(f32[64,256,2,128]{3,1,2,0:T(8,128)} %convolution_bitcast_fusion.1) | data formatting | bytes 33554432 | tf_op jit(solution)/shard_map/pkqj,qajw->pakw/dot_general | solution.py:55
  451.7 7.9 subtract_convert_fusion.2
  464.5 11.4 %copy.84 = bf16[2,64,128,256]{3,2,1,0:T(8,128)(2,1)} copy(bf16[2,64,128,256]{3,1,2,0:T(8,128)(2,1)} %fusion.1) | data formatting | bytes 16777216 | tf_op jit(solution)/shard_map/convert_element_type | solution.py:137
  475.9 14.5 %copy.85 = bf16[2,8192,256]{2,0,1:T(2,128)(2,1)S(1)} copy(bf16[2,8192,256]{2,1,0:T(8,128)(2,1)} %bitcast.207) | data formatting | bytes 16777216 | tf_op jit(solution)/shard_map/convert_element_type | solution.py:137
  490.4 167.5 %all_to_all.30 = bf16[2,8192,256]{2,0,1:T(2,128)(2,1)} all-to-all(bf16[2,8192,256]{2,0,1:T(2,128)(2,1)S(1)} %copy.85), channel_id=1, replica_groups=mesh['rows'=32,'mask'=8] {'rows'}, dimensions={1} | all-to-all | bytes 16777216 | tf_op jit(solution)/shard_map/all_to_all | solution.py:138
  665.6 12.0 %copy.87 = bf16[2,256,32,256]{1,3,2,0:T(8,128)(2,1)} copy(bf16[2,256,32,256]{3,1,2,0:T(8,128)(2,1)} %bitcast.208) | data formatting | bytes 16777216 | tf_op jit(solution)/shard_map/all_to_all | solution.py:138
  677.6 12.0 %copy.105 = bf16[2,256,64,128,1]{3,2,0,1,4:T(8,128)(2,1)} copy(bf16[2,256,64,128,1]{1,3,2,0,4:T(8,128)(2,1)} %bitcast.209) | data formatting | bytes 16777216 | tf_op jit(solution)/shard_map/reshape.18
  704.7 20.0 %mul.910 = f32[1,2,256,8192]{3,1,2,0:T(2,128)} reshape(f32[1,2,256,64,128]{4,3,1,2,0:T(8,128)} %fusion) | data formatting | bytes 33554432 | tf_op jit(solution)/shard_map/mul | solution.py:81
  724.7 21.0 %fusion.96 = (f32[1,1,256,8192]{3,1,2,0:T(1,128)S(1)}, f32[1,1,256,8192]{3,1,2,0:T(1,128)}) fusion(f32[1,2,256,8192]{3,1,2,0:T(2,128)} %mul.910), kind=kLoop, calls=%fused_computation.162 | loop fusion | bytes 33554432 | tf_op jit(solution)/shard_map/slice | solution.py:140
  745.8 20.7 %subtract_convert_fusion = (bf16[1,256,8192]{2,1,0:T(8,128)(2,1)S(1)}, bf16[1,256,8192]{2,1,0:T(8,128)(2,1)}) fusion(f32[1,1,256,8192]{3,1,2,0:T(1,128)} %get-tuple-element.14, f32[1,1,256,8192]{3,1,2,0:T(1,128)S(1)} %get-tuple-element.13, s32[]{:T(128)} %bitcast.8, s32[8192]{0:T(1024)S(1)} %copy-done.2, s32[256]{0:T(256)S(1)} %copy-done.4), kind=kLoop, calls=%fused_computation.58 | loop fusion | flops 58720256 | bytes 25199620 | tf_op jit(solution)/shard_map/convert.1
  772.7 211.5 %psum.7 = f32[]{:T(128)} all-reduce(f32[]{:T(128)} %get-tuple-element.2), channel_id=1, replica_groups=mesh['rows'=32,'mask'=8] {'rows','mask'}, use_global_device_ids=true, to_apply=%region_2.3 | all-reduce | flops 1 | bytes 8 | tf_op jit(solution)/shard_map/psum | solution.py:147
  (48 shorter events, 91.8 us)
Async XLA Ops:
  7.2 101.0 %all-gather.2.cloned.1.call-start = ((), (), s32[]{:S(2)}) async-start(), calls=%async_computation.3 | async-start | bytes 9437184 | tf_op jit(solution)/shard_map/all_gather | solution.py:105
  8.6 109.4 %copy-start.3 = (s32[256]{0:T(256)}, s32[256]{0:T(256)S(1)}, u32[]{:S(2)}) copy-start(s32[256]{0:T(256)S(1)} %add_multiply_fusion) | copy-start | bytes 3076
  9.0 108.9 %copy-start.1 = (s32[8192]{0:T(1024)}, s32[8192]{0:T(1024)S(1)}, u32[]{:S(2)}) copy-start(s32[8192]{0:T(1024)S(1)} %iota_multiply_fusion) | copy-start | bytes 98308
  180.1 159.3 %all-to-all-start = ((bf16[2,256,8192]{1,0,2:T(2,128)(2,1)}), bf16[2,256,8192]{1,0,2:T(2,128)(2,1)}, u32[]{:S(2)}, u32[]{:S(2)}) async-start(bf16[2,256,8192]{1,0,2:T(2,128)(2,1)} %copy.72), calls=%async_computation | async-start | bytes 16777216 | tf_op jit(solution)/shard_map/all_to_all | solution.py:127
  189.6 795.3 %reduce-scatter.2.cloned.1.call-start = ((), (), s32[]{:S(2)}) async-start(), calls=%async_computation.4 | async-start | bytes 9437184 | tf_op jit(solution)/shard_map/reduce_scatter | solution.py:141
  390.4 6.6 copy-start
  724.7 21.1 %copy-start.2 = (s32[8192]{0:T(1024)S(1)}, s32[8192]{0:T(1024)}, u32[]{:S(2)}) copy-start(s32[8192]{0:T(1024)} %copy-done.1) | copy-start | bytes 98308
  724.7 21.1 %copy-start.4 = (s32[256]{0:T(256)S(1)}, s32[256]{0:T(256)}, u32[]{:S(2)}) copy-start(s32[256]{0:T(256)} %copy-done.3) | copy-start | bytes 3076
Sparse Core Ops, SparseCore 0:
  9.8 98.3 all-gather.1
  772.8 152.2 reduce-scatter.1
where the time goes:
time: 1010 us; the launch traced here: 996 us
  blocking collectives  379 us (38%)
  waiting for transfers between devices  248 us (25%)
  local copies, waits for them, and re-layouts  184 us (18%)
  other arithmetic  88.1 us (9%)
  matrix products  70.1 us (7%)
  between operations  17.2 us (2%)
    psum x1, blocking collectives, shards(): loss_total = lax.psum(loss_part, ('rows', 'mask'))  212 us
    all_to_all x1, blocking collectives, shards(): lax.all_to_all(returning, 'rows', split_axis=1, concat_axis=2, tiled=True)  168 us
    all_to_all x1, waiting for transfers between devices, shards(): lax.all_to_all(outgoing, 'rows', split_axis=2, concat_axis=1, tiled=True)  149 us
    all_gather x1, waiting for transfers between devices, shards(): slab = lax.all_gather(image_field, 'mask', axis=1, tiled=True)  98.1 us
    dot_general x8, matrix products, factor(): return jnp.einsum(form, table, values, preferred_element_type=jnp.float32)  70.1 us
    another operation x9, other arithmetic  35.3 us
    convert_element_type x2, local copies, waits for them, and re-layouts, shards(): returning = cols_inverse(weighted, inverse_tables).astype(jnp.bfloat16)  25.9 us
    convert_element_type x2, local copies, waits for them, and re-layouts, shards(): rows_forward(masked[None], forward_tables)[0].astype(jnp.bfloat16)  24.1 us
  transfers between devices with their start and end apart: 3, of which 2 were waited for; matrix products, arithmetic and copies ran while one was open for 0% of the time, Pallas kernels for 0%

commit v1 on v0

--- a/solution.py
+++ b/solution.py
@@ -102,7 +102,15 @@
 
 
 def shards(image_field, amplitudes, mask_ids):
-    slab = lax.all_gather(image_field, "mask", axis=1, tiled=True)
+    slab = jnp.concatenate(
+        lax.all_to_all(
+            jnp.stack([image_field] * lax.axis_size("mask")),
+            axis_name="mask",
+            split_axis=0,
+            concat_axis=0,
+        ),
+        1,
+    )
     slab_rows = slab.shape[1]
     width = slab.shape[2]
     outer = width // INNER

time: 1010 us -> 1040 us (1.030)
  blocking collectives: 379 us -> 185 us
  waiting for transfers between devices: 248 us -> 409 us
  starting transfers between devices: 9.93 us -> 49.4 us
  local copies, waits for them, and re-layouts: 184 us -> 198 us
  other arithmetic: 88.1 us -> 101 us
    all_to_all x0 -> x2, waiting for transfers between devices: none -> 265 us  [the longest x1 174 us: shards(): lax.all_to_all(returning, 'rows', split_axis=1, concat_axis=2, tiled=True)]
    all_to_all x1 -> x0, blocking collectives: 168 us -> none  [shards(): lax.all_to_all(returning, 'rows', split_axis=1, concat_axis=2, tiled=True)]
    all_gather x1 -> x0, waiting for transfers between devices: 98.1 us -> none  [shards(): slab = lax.all_gather(image_field, 'mask', axis=1, tiled=True)]
    all_to_all x0 -> x2, starting transfers between devices: none -> 37.4 us  [the longest x1 31 us: shards(): lax.all_to_all(returning, 'rows', split_axis=1, concat_axis=2, tiled=True)]
    psum x1, blocking collectives: 212 us -> 185 us  [shards(): loss_total = lax.psum(loss_part, ('rows', 'mask'))]
    convert_element_type x0 -> x1, other arithmetic: none -> 11.4 us  [shards(): slab[0].astype(jnp.float32)]
    another operation x9 -> x10, other arithmetic: 35.3 us -> 46.4 us
  transfers between devices with their start and end apart: 3 -> 4, of which waited for: 2 -> 3; matrix products, arithmetic and copies ran while one was open for 0% -> 0% of each run, Pallas kernels for 0% -> 0%
where the time goes in v1:
time: 1040 us; the launch traced here: 1030 us
  waiting for transfers between devices  409 us (39%)
  local copies, waits for them, and re-layouts  198 us (19%)
  blocking collectives  185 us (18%)
  other arithmetic  101 us (10%)
  matrix products  70.2 us (7%)
  starting transfers between devices  49.4 us (5%)
  between operations  17.2 us (2%)
    psum x1, blocking collectives, shards(): loss_total = lax.psum(loss_part, ('rows', 'mask'))  185 us
    all_to_all x1, waiting for transfers between devices, shards(): lax.all_to_all(returning, 'rows', split_axis=1, concat_axis=2, tiled=True)  174 us
    all_to_all x1, waiting for transfers between devices, shards(): lax.all_to_all(outgoing, 'rows', split_axis=2, concat_axis=1, tiled=True)  143 us
    all_to_all x1, waiting for transfers between devices, shards(): lax.all_to_all(jnp.stack([image_field] * lax.axis_size('mask')), axis_nam...  90.9 us
    dot_general x8, matrix products, factor(): return jnp.einsum(form, table, values, preferred_element_type=jnp.float32)  70.2 us
    another operation x10, other arithmetic  46.4 us
    all_to_all x1, starting transfers between devices, shards(): lax.all_to_all(returning, 'rows', split_axis=1, concat_axis=2, tiled=True)  31 us
    convert_element_type x2, local copies, waits for them, and re-layouts, shards(): returning = cols_inverse(weighted, inverse_tables).astype(jnp.bfloat16)  27.8 us
  transfers between devices with their start and end apart: 4, of which 3 were waited for; matrix products, arithmetic and copies ran while one was open for 0% of the time, Pallas kernels for 0%

profile of v1, /device:TPU:1, one launch (start us, length us, event | category | flops | bytes accessed | tf_op | source)
XLA Modules:
  0.0 1029.8 jit_solution(8829209151510997980)
XLA Ops:
  21.9 90.9 %all-to-all-done = bf16[8,2,32,8192]{3,2,1,0:T(8,128)(2,1)} async-done(((bf16[8,2,32,8192]{3,2,1,0:T(8,128)(2,1)}), bf16[8,2,32,8192]{3,2,1,0:T(8,128)(2,1)}, u32[]{:S(2)}, u32[]{:S(2)}) %all-to-all-start) | async-done | bytes 8388640 | tf_op jit(solution)/shard_map/all_to_all | solution.py:106
  112.7 11.4 %slice_convert_fusion.1 = (f32[1,8,32,8192]{3,2,0,1:T(8,128)}, f32[1,8,32,8192]{3,2,0,1:T(8,128)}) fusion(bf16[2,8,32,8192]{3,2,0,1:T(8,128)(2,1)} %bitcast.8), kind=kLoop, calls=%fused_computation.93 | loop fusion | flops 4194304 | bytes 25165824 | tf_op jit(solution)/shard_map/convert_element_type | solution.py:131
  134.8 11.1 %fusion.14 = (bf16[1,256,64,128]{3,2,0,1:T(8,128)(2,1)S(1)}, bf16[1,256,64,128]{3,2,0,1:T(8,128)(2,1)}) fusion(f32[32,8,64,128]{3,2,1,0:T(8,128)S(1)} %copy.123, f32[32,8,64,128]{3,2,1,0:T(8,128)} %copy.122, s32[]{:T(128)} %bitcast.9, s32[64,128]{1,0:T(8,128)S(1)} %add_multiply_fusion, s32[256]{0:T(256)S(1)} %add_multiply_fusion.1), kind=kLoop, calls=%fused_computation.28 | loop fusion | flops 56623104 | bytes 25199620 | tf_op jit(solution)/shard_map/convert.37
  162.8 16.8 %fusion.47 = bf16[1,2,256,64,128]{2,4,1,3,0:T(8,128)(2,1)} fusion(bf16[2,256,64,128,1]{3,2,1,0,4:T(8,128)(2,1)} %maximum_bitcast_fusion.2, bf16[1,128,2,128]{3,1,2,0:T(8,128)(2,1)S(1)} %get-tuple-element.23, bf16[1,128,2,128]{3,1,2,0:T(8,128)(2,1)S(1)} %get-tuple-element.24), kind=kOutput, calls=%fused_computation.87 | convolution fusion | flops 2156134400 | bytes 16908288 | tf_op jit(solution)/shard_map/pkqj,xqraj->xprak/dot_general | solution.py:55
  187.3 16.4 %copy.72 = bf16[2,256,8192]{1,0,2:T(2,128)(2,1)} copy(bf16[2,256,8192]{1,2,0:T(8,128)(2,1)} %bitcast.226) | data formatting | bytes 16777216 | tf_op jit(solution)/shard_map/convert_element_type | solution.py:134
  203.7 12.0 %all-to-all-start.1 = ((bf16[2,256,8192]{1,0,2:T(2,128)(2,1)}), bf16[2,256,8192]{1,0,2:T(2,128)(2,1)}, u32[]{:S(2)}, u32[]{:S(2)}) async-start(bf16[2,256,8192]{1,0,2:T(2,128)(2,1)} %copy.72), calls=%async_computation.1 | async-start | bytes 16777216 | tf_op jit(solution)/shard_map/all_to_all | solution.py:135
  216.1 143.4 %all-to-all-done.1 = bf16[2,256,8192]{1,0,2:T(2,128)(2,1)} async-done(((bf16[2,256,8192]{1,0,2:T(2,128)(2,1)}), bf16[2,256,8192]{1,0,2:T(2,128)(2,1)}, u32[]{:S(2)}, u32[]{:S(2)}) %all-to-all-start.1) | async-done | bytes 8388640 | tf_op jit(solution)/shard_map/all_to_all | solution.py:135
  367.2 12.0 %copy.74 = bf16[2,32,256,256]{3,2,1,0:T(8,128)(2,1)} copy(bf16[2,32,256,256]{2,3,1,0:T(8,128)(2,1)} %bitcast.227) | data formatting | bytes 16777216 | tf_op jit(solution)/shard_map/all_to_all | solution.py:135
  379.2 9.7 fusion.42
  400.6 10.2 fusion.2
  417.3 12.7 %fusion.6 = (f32[]{:T(128)}, bf16[1,8192,256]{2,1,0:T(8,128)(2,1)}, bf16[1,8192,256]{2,1,0:T(8,128)(2,1)}) fusion(bf16[1,8192,256]{2,1,0:T(8,128)(2,1)S(1)} %copy-done.1, f32[1,8192,256]{2,1,0:T(8,128)} %bitcast.232, f32[1,8192,256]{2,1,0:T(8,128)} %bitcast.231), kind=kLoop, calls=%fused_computation.18 | loop fusion | flops 29360128 | bytes 29360132 | tf_op jit(solution)/shard_map/reduce_sum | solution.py:143
  442.9 11.6 %convolution_bitcast_fusion.1 = f32[64,256,2,128]{3,1,2,0:T(8,128)} fusion(bf16[1,64,128,256]{2,3,0,1:T(8,128)(2,1)} %copy.80, bf16[1,64,128,256]{2,3,0,1:T(8,128)(2,1)} %copy.79, bf16[1,128,2,128]{3,1,2,0:T(8,128)(2,1)S(1)} %get-tuple-element.22, bf16[1,128,2,128]{3,1,2,0:T(8,128)(2,1)S(1)} %get-tuple-element.21), kind=kOutput, calls=%fused_computation.15 | convolution fusion | flops 2164523008 | bytes 25296896 | tf_op jit(solution)/shard_map/pkqj,qajw->pakw/dot_general | solution.py:55
  454.5 17.4 %copy.81 = f32[64,256,2,128]{1,0,3,2:T(8,128)} copy(f32[64,256,2,128]{3,1,2,0:T(8,128)} %convolution_bitcast_fusion.1) | data formatting | bytes 33554432 | tf_op jit(solution)/shard_map/pkqj,qajw->pakw/dot_general | solution.py:55
  471.9 7.9 subtract_convert_fusion.2
  484.7 11.4 %copy.84 = bf16[2,64,128,256]{3,2,1,0:T(8,128)(2,1)} copy(bf16[2,64,128,256]{3,1,2,0:T(8,128)(2,1)} %fusion.1) | data formatting | bytes 16777216 | tf_op jit(solution)/shard_map/convert_element_type | solution.py:145
  496.2 16.4 %copy.85 = bf16[2,8192,256]{2,0,1:T(2,128)(2,1)} copy(bf16[2,8192,256]{2,1,0:T(8,128)(2,1)} %bitcast.228) | data formatting | bytes 16777216 | tf_op jit(solution)/shard_map/convert_element_type | solution.py:145
  512.5 31.0 %all-to-all-start.2 = ((bf16[2,8192,256]{2,0,1:T(2,128)(2,1)}), bf16[2,8192,256]{2,0,1:T(2,128)(2,1)}, u32[]{:S(2)}, u32[]{:S(2)}) async-start(bf16[2,8192,256]{2,0,1:T(2,128)(2,1)} %copy.85), calls=%async_computation.2 | async-start | bytes 16777216 | tf_op jit(solution)/shard_map/all_to_all | solution.py:146
  543.6 174.4 %all-to-all-done.2 = bf16[2,8192,256]{2,0,1:T(2,128)(2,1)} async-done(((bf16[2,8192,256]{2,0,1:T(2,128)(2,1)}), bf16[2,8192,256]{2,0,1:T(2,128)(2,1)}, u32[]{:S(2)}, u32[]{:S(2)}) %all-to-all-start.2) | async-done | bytes 8388640 | tf_op jit(solution)/shard_map/all_to_all | solution.py:146
  725.7 12.3 %copy.87 = bf16[2,256,32,256]{1,3,2,0:T(8,128)(2,1)} copy(bf16[2,256,32,256]{3,1,2,0:T(8,128)(2,1)} %bitcast.229) | data formatting | bytes 16777216 | tf_op jit(solution)/shard_map/all_to_all | solution.py:146
  737.9 12.0 %copy.105 = bf16[2,256,64,128,1]{3,2,0,1,4:T(8,128)(2,1)} copy(bf16[2,256,64,128,1]{1,3,2,0,4:T(8,128)(2,1)} %bitcast.230) | data formatting | bytes 16777216 | tf_op jit(solution)/shard_map/reshape.25
  765.0 20.0 %mul.951 = f32[1,2,256,8192]{3,1,2,0:T(2,128)} reshape(f32[1,2,256,64,128]{4,3,1,2,0:T(8,128)} %fusion) | data formatting | bytes 33554432 | tf_op jit(solution)/shard_map/mul | solution.py:81
  785.1 20.9 %fusion.100 = (f32[1,1,256,8192]{3,1,2,0:T(1,128)S(1)}, f32[1,1,256,8192]{3,1,2,0:T(1,128)}) fusion(f32[1,2,256,8192]{3,1,2,0:T(2,128)} %mul.951), kind=kLoop, calls=%fused_computation.173 | loop fusion | bytes 33554432 | tf_op jit(solution)/shard_map/slice | solution.py:148
  806.0 20.7 %subtract_convert_fusion = (bf16[1,256,8192]{2,1,0:T(8,128)(2,1)S(1)}, bf16[1,256,8192]{2,1,0:T(8,128)(2,1)}) fusion(f32[1,1,256,8192]{3,1,2,0:T(1,128)} %get-tuple-element.16, f32[1,1,256,8192]{3,1,2,0:T(1,128)S(1)} %get-tuple-element.15, s32[]{:T(128)} %bitcast.9, s32[8192]{0:T(1024)S(1)} %iota_multiply_fusion, s32[256]{0:T(256)S(1)} %copy-done.5), kind=kLoop, calls=%fused_computation.63 | loop fusion | flops 58720256 | bytes 25199620 | tf_op jit(solution)/shard_map/convert.3
  833.0 185.0 %psum.7 = f32[]{:T(128)} all-reduce(f32[]{:T(128)} %get-tuple-element.2), channel_id=1, replica_groups=mesh['rows'=32,'mask'=8] {'rows','mask'}, use_global_device_ids=true, to_apply=%region_2.3 | all-reduce | flops 1 | bytes 8 | tf_op jit(solution)/shard_map/psum | solution.py:155
  (53 shorter events, 125.0 us)
Async XLA Ops:
  12.7 100.0 %all-to-all-start = ((bf16[8,2,32,8192]{3,2,1,0:T(8,128)(2,1)}), bf16[8,2,32,8192]{3,2,1,0:T(8,128)(2,1)}, u32[]{:S(2)}, u32[]{:S(2)}) async-start(bf16[8,2,32,8192]{3,2,1,0:T(8,128)(2,1)} %stack.167), calls=%async_computation | async-start | bytes 16777216 | tf_op jit(solution)/shard_map/all_to_all | solution.py:106
  19.7 115.1 %copy-start.4 = (s32[256]{0:T(256)}, s32[256]{0:T(256)S(1)}, u32[]{:S(2)}) copy-start(s32[256]{0:T(256)S(1)} %add_multiply_fusion.1) | copy-start | bytes 3076
  124.2 5.8 copy-start
  203.7 155.8 %all-to-all-start.1 = ((bf16[2,256,8192]{1,0,2:T(2,128)(2,1)}), bf16[2,256,8192]{1,0,2:T(2,128)(2,1)}, u32[]{:S(2)}, u32[]{:S(2)}) async-start(bf16[2,256,8192]{1,0,2:T(2,128)(2,1)} %copy.72), calls=%async_computation.1 | async-start | bytes 16777216 | tf_op jit(solution)/shard_map/all_to_all | solution.py:135
  410.8 6.6 copy-start.1
  471.9 7.9 copy-start.2
  471.9 7.9 copy-start.3
  512.5 205.5 %all-to-all-start.2 = ((bf16[2,8192,256]{2,0,1:T(2,128)(2,1)}), bf16[2,8192,256]{2,0,1:T(2,128)(2,1)}, u32[]{:S(2)}, u32[]{:S(2)}) async-start(bf16[2,8192,256]{2,0,1:T(2,128)(2,1)} %copy.85), calls=%async_computation.2 | async-start | bytes 16777216 | tf_op jit(solution)/shard_map/all_to_all | solution.py:146
  543.5 475.1 %reduce-scatter.2.cloned.1.call-start = ((), (), s32[]{:S(2)}) async-start(), calls=%async_computation.4 | async-start | bytes 9437184 | tf_op jit(solution)/shard_map/reduce_scatter | solution.py:149
  785.1 21.0 %copy-start.5 = (s32[256]{0:T(256)S(1)}, s32[256]{0:T(256)}, u32[]{:S(2)}) copy-start(s32[256]{0:T(256)} %copy-done.4) | copy-start | bytes 3076
Sparse Core Ops, SparseCore 0:
  833.1 123.2 reduce-scatter.1
